TPU v7x, 256 devices: a whole 4x4x8 slice. The times are simulated.
256 devices in a mesh: replica: 32 (over x, z), shard: 8 (over y, core).
Axes of the slice: x: 4, y: 4, z: 8, core: 2. Of those that a mesh axis runs over, the one named last changes fastest.
Arguments:
- gradient_table: bfloat16 [32, 4096, 768], P('replica', 'shard'), may hold values from -6 to 6
- error_table: float32 [32, 4096, 768], P('replica', 'shard'), may hold values from -6 to 6
- moment_table: float32 [4096, 768], P('shard'), may hold values from -2 to 2
- weight_table: float32 [4096, 768], P('shard'), may hold values from -3 to 3
- start_table: float32 [768, 32], replicated, may hold values from -0.21875 to 0.21875
- gram_table: float32 [2, 32, 32], replicated, as said below
- gradient_query: bfloat16 [32, 768, 768], P('replica', 'shard'), may hold values from -6 to 6
- error_query: float32 [32, 768, 768], P('replica', 'shard'), may hold values from -6 to 6
- moment_query: float32 [768, 768], P('shard'), may hold values from -2 to 2
- weight_query: float32 [768, 768], P('shard'), may hold values from -3 to 3
- start_query: float32 [768, 32], replicated, may hold values from -0.21875 to 0.21875
- gram_query: float32 [2, 32, 32], replicated, as said below
- gradient_norms: float32 [32, 3840], P('replica', 'shard'), may hold values from -6 to 6
- moment_norms: float32 [3840], P('shard'), may hold values from -2 to 2
- weight_norms: float32 [3840], P('shard'), may hold values from 0.5 to 1.5
Outputs:
- residual_table: float32 [32, 4096, 768], P('replica', 'shard')
- velocity_table: float32 [4096, 768], P('shard')
- updated_table: float32 [4096, 768], P('shard')
- warm_table: float32 [768, 32], replicated
- residual_query: float32 [32, 768, 768], P('replica', 'shard')
- velocity_query: float32 [768, 768], P('shard')
- updated_query: float32 [768, 768], P('shard')
- warm_query: float32 [768, 32], replicated
- velocity_norms: float32 [3840], P('shard')
- updated_norms: float32 [3840], P('shard')
Inputs may be any that keep to these rules, and one draw needn't show every extreme that they name: `gram_table`: each of the two 32 x 32 matrices is symmetric. `gram_query`: each of the two 32 x 32 matrices is symmetric.
All inputs are finite; a program needn't handle non-finite values.
Results may differ from a plain program's by a relative error of at most 0.0003.
Values sent between devices are 32-bit elements; how exact they have to be, the bound alone decides.
No kernel may reach another device: no remote copies, remote signals or barrier semaphores. Data moves between devices by JAX's collectives and lax.ppermute only.
A program may use at most 64 MiB of HBM per device.

v0:
```python
import jax
import jax.numpy as jnp
from jax import lax
from jax.sharding import PartitionSpec as P

decay_rate = 0.9
step_rate = 0.01


def product(left, right):
    return jnp.dot(left, right, precision=lax.Precision.HIGHEST, preferred_element_type=jnp.float32)


def product_rows(left, right):
    return lax.dot_general(
        left,
        right,
        (((0,), (0,)), ((), ())),
        precision=lax.Precision.HIGHEST,
        preferred_element_type=jnp.float32,
    )


def product_outer(left, right):
    return lax.dot_general(
        left,
        right,
        (((1,), (1,)), ((), ())),
        precision=lax.Precision.HIGHEST,
        preferred_element_type=jnp.float32,
    )


def reduce_right(table_part, query_part):
    return lax.psum((table_part, query_part), ("replica", "shard"))


def local(
    gradient_table,
    error_table,
    moment_table,
    weight_table,
    start_table,
    gram_table,
    gradient_query,
    error_query,
    moment_query,
    weight_query,
    start_query,
    gram_query,
    gradient_norms,
    moment_norms,
    weight_norms,
):
    replicas = lax.axis_size("replica")
    merged_table = gradient_table[0].astype(jnp.float32) + error_table[0]
    merged_query = gradient_query[0].astype(jnp.float32) + error_query[0]
    first_sums = lax.psum(
        (product(merged_table, start_table), product(merged_query, start_query), gradient_norms[0]),
        "replica",
    )
    basis_table = product(first_sums[0] / replicas, gram_table[0])
    basis_query = product(first_sums[1] / replicas, gram_query[0])
    mean_norms = first_sums[2] / replicas
    velocity_norms = decay_rate * moment_norms + mean_norms
    updated_norms = weight_norms - step_rate * velocity_norms
    right_sums = reduce_right(
        product_rows(merged_table, basis_table), product_rows(merged_query, basis_query)
    )
    right_table = right_sums[0] / replicas
    right_query = right_sums[1] / replicas
    second_sums = lax.psum(
        (product(merged_table, right_table), product(merged_query, right_query)), "replica"
    )
    basis_table = product(second_sums[0] / replicas, gram_table[1])
    basis_query = product(second_sums[1] / replicas, gram_query[1])
    right_sums = reduce_right(
        product_rows(merged_table, basis_table), product_rows(merged_query, basis_query)
    )
    warm_table = right_sums[0] / replicas
    warm_query = right_sums[1] / replicas
    approx_table = product_outer(basis_table, warm_table)
    approx_query = product_outer(basis_query, warm_query)
    residual_table = (merged_table - approx_table)[None]
    residual_query = (merged_query - approx_query)[None]
    velocity_table = decay_rate * moment_table + approx_table
    velocity_query = decay_rate * moment_query + approx_query
    updated_table = weight_table - step_rate * velocity_table
    updated_query = weight_query - step_rate * velocity_query
    return (
        residual_table,
        velocity_table,
        updated_table,
        warm_table,
        residual_query,
        velocity_query,
        updated_query,
        warm_query,
        velocity_norms,
        updated_norms,
    )


def solution(mesh):
    placed = (
        P("replica", "shard", None),
        P("replica", "shard", None),
        P("shard", None),
        P("shard", None),
        P(),
        P(),
        P("replica", "shard", None),
        P("replica", "shard", None),
        P("shard", None),
        P("shard", None),
        P(),
        P(),
        P("replica", "shard"),
        P("shard"),
        P("shard"),
    )
    return jax.shard_map(
        local,
        mesh=mesh,
        in_specs=placed,
        out_specs=(
            P("replica", "shard", None),
            P("shard", None),
            P("shard", None),
            P(),
            P("replica", "shard", None),
            P("shard", None),
            P("shard", None),
            P(),
            P("shard"),
            P("shard"),
        ),
        check_vma=False,
    )
```

profile of v0, /device:TPU:32, one launch (start us, length us, event | category | flops | bytes accessed | tf_op | source)
XLA Modules:
  0.0 829.3 jit_solution(1121446690353790996)
XLA Ops:
  7.2 0.0 copy-start
  7.2 0.0 copy-start.9
  7.2 0.0 copy-start.3
  7.2 0.0 copy-start.4
  7.2 0.0 copy-start.11
  7.2 0.0 copy-start.12
  7.2 0.0 all-reduce.8.cloned.1.call-start
  7.3 0.8 copy-done
  8.1 3.7 fusion.6
  11.8 0.0 all-reduce.8.cloned.1.call-update
  11.9 0.0 all-reduce.14.cloned.1.call-start
  11.9 0.0 copy-done.9
  11.9 0.0 copy-done.3
  11.9 0.0 copy-done.4
  11.9 0.4 fusion.15
  12.3 140.2 %psum.67 = f32[96,32]{1,0:T(8,128)S(1)} all-reduce(f32[96,32]{1,0:T(8,128)S(1)} %fusion.15), channel_id=1, replica_groups=mesh['replica'=32,'shard'=8] {'replica'}, use_global_device_ids=true, to_apply=%region_4.0 | all-reduce | flops 3072 | bytes 24576 | tf_op jit(solution)/shard_map/psum | solution.py:58
  152.5 0.0 copy-done.11
  152.5 0.2 fusion.28
  152.7 1.0 fusion.13
  153.7 5.7 all-reduce.8.cloned.1.call-done
  159.4 0.0 copy-done.12
  159.4 1.3 fusion.20
  160.7 0.0 copy-done.2
  160.7 1.8 fusion.4
  162.6 0.0 all-reduce.14.cloned.1.call-update
  162.6 0.0 all-reduce.10.cloned.1.call-start
  162.6 249.9 %all-reduce.14.cloned.1.call-done = (f32[768,32]{0,1:T(8,128)}, f32[768,32]{0,1:T(8,128)}) async-done(((f32[768,32]{0,1:T(8,128)}, f32[768,32]{0,1:T(8,128)}), (f32[768,32]{0,1:T(8,128)}, f32[768,32]{0,1:T(8,128)})) %all-reduce.14.cloned.1.call-update) | async-done | bytes 196624 | tf_op jit(solution)/shard_map/psum | solution.py:35
  412.6 3.0 fusion.2
  415.6 0.0 all-reduce.10.cloned.1.call-update
  415.6 0.0 all-reduce.12.cloned.1.call-start
  415.7 0.4 fusion.11
  416.1 136.0 %all-reduce.2 = (f32[96,32]{1,0:T(8,128)S(1)}, f32[480]{0:T(512)S(1)}) all-reduce(f32[96,32]{1,0:T(8,128)S(1)} %fusion.11, f32[480]{0:T(512)S(1)} %bitcast.51), channel_id=1, replica_groups=mesh['replica'=32,'shard'=8] {'replica'}, use_global_device_ids=true, to_apply=%region_6.0 | all-reduce | flops 3552 | bytes 28416 | tf_op jit(solution)/shard_map/psum | solution.py:72
  552.0 0.2 fusion.26
  552.3 1.0 fusion.9
  553.2 8.1 all-reduce.10.cloned.1.call-done
  561.3 1.3 fusion.18
  562.7 1.8 fusion
  564.5 0.0 all-reduce.12.cloned.1.call-update
  564.5 0.6 multiply_subtract_fusion.2
  565.1 249.4 %all-reduce.12.cloned.1.call-done = (f32[768,32]{0,1:T(8,128)}, f32[768,32]{0,1:T(8,128)}) async-done(((f32[768,32]{0,1:T(8,128)}, f32[768,32]{0,1:T(8,128)}), (f32[768,32]{0,1:T(8,128)}, f32[768,32]{0,1:T(8,128)})) %all-reduce.12.cloned.1.call-update) | async-done | bytes 196624 | tf_op jit(solution)/shard_map/psum | solution.py:35
  814.4 1.0 broadcast_multiply_fusion
  815.4 0.0 copy-start.5
  815.4 0.0 copy-start.6
  815.4 0.0 copy-start.7
  815.4 0.0 copy-start.8
  815.5 5.9 multiply_subtract_fusion
  821.3 0.0 copy-done.6
  821.3 1.4 multiply_subtract_fusion.1
  (14 shorter events, 0.0 us)
Async XLA Ops:
  7.2 0.9 copy-start
  7.2 4.7 copy-start.9
  7.2 4.7 copy-start.3
  7.2 4.7 copy-start.4
  7.2 145.3 %copy-start.11 = (f32[2,32,32]{2,1,0:T(8,128)S(1)}, f32[2,32,32]{2,1,0:T(8,128)}, u32[]{:S(2)}) copy-start(f32[2,32,32]{2,1,0:T(8,128)} %param.26) | copy-start | bytes 24580
  7.2 152.2 %copy-start.12 = (f32[2,32,32]{2,1,0:T(8,128)S(1)}, f32[2,32,32]{2,1,0:T(8,128)}, u32[]{:S(2)}) copy-start(f32[2,32,32]{2,1,0:T(8,128)} %param.20) | copy-start | bytes 24580
  7.2 152.2 %all-reduce.8.cloned.1.call-start = ((), (), s32[]{:S(2)}) async-start(), calls=%async_computation | async-start | bytes 524288 | tf_op jit(solution)/shard_map/psum | solution.py:58
  8.1 152.6 %copy-start.2 = (bf16[1,512,768]{2,1,0:T(8,128)(2,1)S(1)}, bf16[1,512,768]{2,1,0:T(8,128)(2,1)}, u32[]{:S(2)}) copy-start(bf16[1,512,768]{2,1,0:T(8,128)(2,1)} %param.15) | copy-start | bytes 2359300
  11.8 148.9 %copy-start.1 = (f32[1,512,768]{2,1,0:T(8,128)S(1)}, f32[1,512,768]{2,1,0:T(8,128)}, u32[]{:S(2)}) copy-start(f32[1,512,768]{2,1,0:T(8,128)} %param.16) | copy-start | bytes 4718596
  11.9 400.7 %all-reduce.14.cloned.1.call-start = ((), (), s32[]{:S(2)}) async-start(), calls=%async_computation.3 | async-start | bytes 393216 | tf_op jit(solution)/shard_map/psum | solution.py:35
  162.6 398.8 %all-reduce.10.cloned.1.call-start = ((), (), s32[]{:S(2)}) async-start(), calls=%async_computation.1 | async-start | bytes 524288 | tf_op jit(solution)/shard_map/psum | solution.py:72
  412.6 3.1 copy-start.10
  412.6 3.5 copy-start.13
  415.6 398.8 %all-reduce.12.cloned.1.call-start = ((), (), s32[]{:S(2)}) async-start(), calls=%async_computation.2 | async-start | bytes 393216 | tf_op jit(solution)/shard_map/psum | solution.py:35
  553.2 11.3 %copy-start.14 = (f32[480]{0:T(512)S(1)}, f32[480]{0:T(512)}, u32[]{:S(2)}) copy-start(f32[480]{0:T(512)} %param.29) | copy-start | bytes 5764
  553.2 11.3 %copy-start.15 = (f32[480]{0:T(512)S(1)}, f32[480]{0:T(512)}, u32[]{:S(2)}) copy-start(f32[480]{0:T(512)} %param.28) | copy-start | bytes 5764
  815.4 5.9 copy-start.5
  815.4 5.9 copy-start.6
  815.4 5.9 copy-start.7
  815.4 5.9 copy-start.8
Sparse Core Ops, SparseCore 0:
  12.1 147.2 all-reduce.7
  165.6 246.9 all-reduce.13
  416.6 144.6 all-reduce.9
  567.4 247.0 all-reduce.11
where the time goes:
time: 832 us; the launch traced here: 829 us
  waiting for transfers between devices  513 us (62%)
  blocking collectives  276 us (33%)
  matrix products  23.3 us (3%)
  between operations  14 us (2%)
    psum x2, waiting for transfers between devices, reduce_right(): return lax.psum((table_part, query_part), ('replica', 'shard'))  499 us
    psum x1, blocking collectives, local(): lax.psum((product(merged_table, start_table), product(merged_query, start...  140 us
    psum x1, blocking collectives, local(): lax.psum((product(merged_table, right_table), product(merged_query, right...  136 us
  transfers between devices with their start and end apart: 4, of which 4 were waited for; matrix products, arithmetic and copies ran while one was open for 0% of the time, Pallas kernels for 0%

commit v1 on v0

v1 whole, which is shorter than its diff:
```python
import jax
import jax.numpy as jnp
from jax import lax
from jax.sharding import PartitionSpec as P

decay_rate = 0.9
step_rate = 0.01
LANES = 128


def dot(left, right, contract):
    return lax.dot_general(
        left,
        right,
        ((contract[0], contract[1]), ((), ())),
        precision=lax.Precision.HIGHEST,
        preferred_element_type=jnp.float32,
    )


def exchange(blocks, axis):
    return lax.all_to_all(blocks, axis, 0, 0)


def spread(block, axis):
    return exchange(jnp.broadcast_to(block[None], (lax.axis_size(axis),) + block.shape), axis)


def local(
    gradient_table,
    error_table,
    moment_table,
    weight_table,
    start_table,
    gram_table,
    gradient_query,
    error_query,
    moment_query,
    weight_query,
    start_query,
    gram_query,
    gradient_norms,
    moment_norms,
    weight_norms,
):
    replicas = lax.axis_size("replica")
    shards = lax.axis_size("shard")
    rows_table, width = moment_table.shape
    rows_query = moment_query.shape[0]
    rank = start_table.shape[1]
    cols = width // LANES
    per_table = rows_table // replicas
    per_query = rows_query // replicas
    entries = moment_norms.shape[0]
    per_norms = entries // replicas

    merged_table = gradient_table[0].astype(jnp.float32) + error_table[0]
    merged_query = gradient_query[0].astype(jnp.float32) + error_query[0]

    def pack(merged, per):
        blocks = merged.reshape(replicas, per, cols, LANES)
        return blocks.transpose(0, 2, 1, 3).reshape(replicas, per * cols, LANES)

    n_table = per_table * cols
    n_query = per_query * cols
    filled = n_table + n_query
    height = -(-(filled + 1) // 8) * 8
    norms = gradient_norms[0].reshape(replicas, 1, per_norms)
    norms = jnp.pad(norms, ((0, 0), (0, height - filled - 1), (0, LANES - per_norms)))
    sent = jnp.concatenate([pack(merged_table, per_table), pack(merged_query, per_query), norms], axis=1)
    own = jnp.sum(exchange(sent, "replica"), axis=0)

    rows = spread(own, "shard")

    def unpack(part, per):
        blocks = part.reshape(shards, cols, per, LANES).transpose(0, 2, 1, 3)
        return blocks.reshape(shards * per, width)

    sum_table = unpack(rows[:, :n_table], per_table)
    sum_query = unpack(rows[:, n_table:filled], per_query)

    tall = 16
    stack = 2 * rank // tall
    used = cols * stack

    def reduce_right(basis_table, basis_query):
        right = jnp.concatenate(
            [dot(basis_table, sum_table, ((0,), (0,))), dot(basis_query, sum_query, ((0,), (0,)))], axis=0
        )
        blocks = right.reshape(stack, tall, cols, LANES).transpose(2, 0, 1, 3).reshape(used, tall, LANES)
        blocks = jnp.pad(blocks, ((0, replicas - used), (0, 0), (0, 0)))
        return jnp.sum(exchange(blocks, "replica"), axis=0) / replicas

    def stacked(blocks):
        blocks = blocks[:used].reshape(cols, stack, tall, LANES).transpose(1, 2, 0, 3)
        return blocks.reshape(2 * rank, width)

    basis_table = dot(dot(sum_table, start_table, ((1,), (0,))) / replicas, gram_table[0], ((1,), (0,)))
    basis_query = dot(dot(sum_query, start_query, ((1,), (0,))) / replicas, gram_query[0], ((1,), (0,)))
    right = stacked(spread(reduce_right(basis_table, basis_query), "replica"))
    basis_table = dot(dot(sum_table, right[:rank], ((1,), (1,))) / replicas, gram_table[1], ((1,), (0,)))
    basis_query = dot(dot(sum_query, right[rank:], ((1,), (1,))) / replicas, gram_query[1], ((1,), (0,)))

    shard = lax.axis_index("shard")
    high_table = per_table * rank // LANES
    mine_table = lax.dynamic_slice_in_dim(basis_table, shard * per_table, per_table, 0).reshape(high_table, LANES)
    mine_query = lax.dynamic_slice_in_dim(basis_query, shard * per_query, per_query, 0).reshape(1, per_query * rank)
    mine_query = jnp.pad(mine_query, ((0, 0), (0, LANES - per_query * rank)))
    mine_norms = own[filled : filled + 1]
    mine = jnp.concatenate([reduce_right(basis_table, basis_query), mine_table, mine_query, mine_norms], axis=0)
    mine = jnp.pad(mine, ((0, -mine.shape[0] % 8), (0, 0)))
    final = spread(mine, "replica")

    warm = stacked(final[:, :tall])
    basis_table = final[:, tall : tall + high_table].reshape(rows_table, rank)
    basis_query = final[:, tall + high_table, : per_query * rank].reshape(rows_query, rank)
    mean_norms = final[:, tall + high_table + 1, :per_norms].reshape(entries) / replicas

    velocity_norms = decay_rate * moment_norms + mean_norms
    updated_norms = weight_norms - step_rate * velocity_norms
    approx_table = dot(basis_table, warm[:rank], ((1,), (0,)))
    approx_query = dot(basis_query, warm[rank:], ((1,), (0,)))
    velocity_table = decay_rate * moment_table + approx_table
    velocity_query = decay_rate * moment_query + approx_query
    return (
        (merged_table - approx_table)[None],
        velocity_table,
        weight_table - step_rate * velocity_table,
        warm[:rank].T,
        (merged_query - approx_query)[None],
        velocity_query,
        weight_query - step_rate * velocity_query,
        warm[rank:].T,
        velocity_norms,
        updated_norms,
    )


def solution(mesh):
    per_replica = P("replica", "shard", None)
    per_shard = P("shard", None)
    matrix = (per_replica, per_replica, per_shard, per_shard, P(), P())
    return jax.shard_map(
        local,
        mesh=mesh,
        in_specs=matrix + matrix + (P("replica", "shard"), P("shard"), P("shard")),
        out_specs=(per_replica, per_shard, per_shard, P()) * 2 + (P("shard"), P("shard")),
        check_vma=False,
    )
```

time: 832 us -> 170 us (0.20)
  waiting for transfers between devices: 513 us -> 10.7 us
  blocking collectives: 276 us -> 123 us
  local copies, waits for them, and re-layouts: 0.86 us -> 14.2 us
  between operations: 14 us -> 1.11 us
  matrix products: 23.3 us -> 11 us
    psum x4 -> x0, waiting for transfers between devices: 513 us -> none  [the longest x2 499 us: reduce_right(): return lax.psum((table_part, query_part), ('replica', 'shard'))]
    psum x2 -> x0, blocking collectives: 276 us -> none  [the longest x1 140 us: local(): lax.psum((product(merged_table, start_table), product(merged_query, start...]
    all_to_all x0 -> x5, blocking collectives: none -> 123 us  [exchange(): return lax.all_to_all(blocks, axis, 0, 0)]
    dot_general x14, matrix products: 23.3 us -> 11 us  [dot(): lax.dot_general(left, right, ((contract[0], contract[1]), ((), ())), prec...]
    all_to_all x0 -> x1, waiting for transfers between devices: none -> 10.7 us  [exchange(): return lax.all_to_all(blocks, axis, 0, 0)]
  transfers between devices with their start and end apart: 4 -> 1, of which waited for: 4 -> 1; matrix products, arithmetic and copies ran while one was open for 0% -> 0% of each run, Pallas kernels for 0% -> 0%
where the time goes in v1:
time: 170 us
  blocking collectives  123 us (72%)
  local copies, waits for them, and re-layouts  14.2 us (8%)
  matrix products  11 us (6%)
  waiting for transfers between devices  10.7 us (6%)
  other arithmetic  5.17 us (3%)
  starting transfers between devices  4.56 us (3%)
    all_to_all x5, blocking collectives, exchange(): return lax.all_to_all(blocks, axis, 0, 0)  123 us
    dot_general x14, matrix products, dot(): lax.dot_general(left, right, ((contract[0], contract[1]), ((), ())), prec...  11 us
    all_to_all x1, waiting for transfers between devices, exchange(): return lax.all_to_all(blocks, axis, 0, 0)  10.7 us
    all_to_all x1, starting transfers between devices, exchange(): return lax.all_to_all(blocks, axis, 0, 0)  4.56 us
  transfers between devices with their start and end apart: 1, of which 1 were waited for; matrix products, arithmetic and copies ran while one was open for 0% of the time, Pallas kernels for 0%

profile of v1, /device:TPU:32, one launch (start us, length us, event | category | flops | bytes accessed | tf_op | source)
XLA Modules:
  0.0 169.7 jit_solution(9451019206269592232)
XLA Ops:
  0.7 0.5 broadcast.62
  1.2 1.3 reduce.11
  2.5 0.1 reshape_squeeze.7
  2.6 1.0 convert_add_fusion.1
  3.8 0.9 copy.53
  4.7 0.1 copy-done.7
  4.9 0.2 convert_add_fusion
  5.1 1.6 add.47
  6.6 1.9 %copy.50 = f32[32,6,16,128]{3,2,1,0:T(8,128)S(1)} copy(f32[32,6,16,128]{3,1,2,0:T(8,128)} %bitcast.108) | data formatting | bytes 3145728 | tf_op jit(solution)/shard_map/transpose | solution.py:62
  8.6 0.1 select_maximum_fusion
  8.7 59.5 %all_to_all.30 = f32[32,120,128]{2,1,0:T(8,128)} all-to-all(f32[32,120,128]{2,1,0:T(8,128)S(1)} %select_maximum_fusion), channel_id=1, replica_groups=mesh['replica'=32,'shard'=8] {'replica'}, dimensions={0} | all-to-all | bytes 3932160 | tf_op jit(solution)/shard_map/all_to_all | solution.py:22
  68.2 1.7 reduce_sum.27
  69.9 14.2 %all_to_all.31 = f32[8,120,128]{2,1,0:T(8,128)S(1)} all-to-all(f32[8,120,128]{2,1,0:T(8,128)S(1)} %broadcast_in_dim.10), channel_id=1, replica_groups=mesh['replica'=32,'shard'=8] {'shard'}, dimensions={0} | all-to-all | bytes 983040 | tf_op jit(solution)/shard_map/all_to_all | solution.py:22
  84.2 0.2 convolution_multiply_fusion.3
  84.5 0.1 fusion.37
  84.6 0.3 fusion.25
  84.9 0.1 copy.54
  85.1 0.5 convolution_multiply_fusion.1
  85.6 0.2 fusion.39
  85.8 0.4 fusion.4
  86.3 16.8 %all_to_all.32 = f32[32,16,128]{2,1,0:T(8,128)S(1)} all-to-all(f32[32,16,128]{2,1,0:T(8,128)S(1)} %pad.20), channel_id=1, replica_groups=mesh['replica'=32,'shard'=8] {'replica'}, dimensions={0} | all-to-all | bytes 524288 | tf_op jit(solution)/shard_map/all_to_all | solution.py:22
  103.2 15.6 %all_to_all.33 = f32[32,16,128]{2,1,0:T(8,128)S(1)} all-to-all(f32[32,16,128]{2,1,0:T(8,128)S(1)} %broadcast_in_dim.11), channel_id=1, replica_groups=mesh['replica'=32,'shard'=8] {'replica'}, dimensions={0} | all-to-all | bytes 524288 | tf_op jit(solution)/shard_map/all_to_all | solution.py:22
  118.8 0.1 copy.58
  118.9 0.5 convolution_multiply_fusion
  119.4 0.2 fusion.35
  119.6 0.4 fusion.1
  119.9 0.1 copy.59
  120.0 0.2 convolution_multiply_fusion.2
  120.2 0.2 fusion.33
  120.4 0.3 fusion.22
  120.8 0.7 pad.21
  121.5 4.6 %all-to-all-start.4 = ((f32[32,16,128]{2,1,0:T(8,128)}), f32[32,16,128]{2,1,0:T(8,128)S(1)}, u32[]{:S(2)}, u32[]{:S(2)}) async-start(f32[32,16,128]{2,1,0:T(8,128)} %pad.21), calls=%async_computation.4 | async-start | bytes 524288 | tf_op jit(solution)/shard_map/all_to_all | solution.py:22
  126.1 0.1 constant_dynamic-slice_fusion.1
  126.2 0.1 copy.61
  126.2 0.1 reshape.103
  126.3 0.1 reshape.104
  126.4 10.7 %all-to-all-done.4 = f32[32,16,128]{2,1,0:T(8,128)S(1)} async-done(((f32[32,16,128]{2,1,0:T(8,128)}), f32[32,16,128]{2,1,0:T(8,128)S(1)}, u32[]{:S(2)}, u32[]{:S(2)}) %all-to-all-start.4) | async-done | bytes 262176 | tf_op jit(solution)/shard_map/all_to_all | solution.py:22
  137.3 16.8 %all_to_all.34 = f32[32,24,128]{2,1,0:T(8,128)S(1)} all-to-all(f32[32,24,128]{2,1,0:T(8,128)S(1)} %broadcast_in_dim.12), channel_id=1, replica_groups=mesh['replica'=32,'shard'=8] {'replica'}, dimensions={0} | all-to-all | bytes 786432 | tf_op jit(solution)/shard_map/all_to_all | solution.py:22
  154.1 0.1 div.34
  154.3 0.7 reshape_squeeze.8
  155.1 0.7 copy.63
  155.8 0.7 copy.62
  156.5 1.5 slice.90
  158.0 1.7 reshape.105
  159.7 1.7 %bitcast_bitcast_fusion = (f32[768,32]{0,1:T(8,128)}, f32[768,32]{0,1:T(8,128)}) fusion(f32[4,8,6,128]{3,2,1,0:T(8,128)} %bitcast.125, f32[4,8,6,128]{3,2,1,0:T(8,128)} %bitcast.123), kind=kLoop, calls=%fused_computation.28 | loop fusion | bytes 393216 | tf_op jit(solution)/shard_map/transpose | solution.py:133
  161.4 0.6 multiply_subtract_fusion.2
  162.0 2.5 %multiply_subtract_fusion.1 = (f32[96,768]{1,0:T(8,128)}, f32[96,768]{1,0:T(8,128)}, f32[1,96,768]{2,1,0:T(8,128)}) fusion(f32[96,768]{1,0:T(8,128)} %param.24, f32[96,768]{1,0:T(8,128)} %param.23, f32[1,96,768]{2,1,0:T(8,128)S(1)} %convert_add_fusion.1, f32[96,32]{1,0:T(8,128)} %reshape_squeeze.8, f32[4,8,6,128]{3,2,1,0:T(8,128)} %bitcast.126), kind=kOutput, calls=%fused_computation.19 | convolution fusion | flops 28680192 | bytes 1880064 | tf_op jit(solution)/shard_map/dot_general | solution.py:12
  164.5 5.2 %multiply_subtract_fusion = (f32[512,768]{1,0:T(8,128)}, f32[512,768]{1,0:T(8,128)}, f32[1,512,768]{2,1,0:T(8,128)}) fusion(f32[512,768]{1,0:T(8,128)S(1)} %copy-done.1, f32[512,768]{1,0:T(8,128)} %param.17, f32[1,512,768]{2,1,0:T(8,128)S(1)} %convert_add_fusion, f32[512,32]{1,0:T(8,128)S(1)} %copy-done.5, f32[4,8,6,128]{3,2,1,0:T(8,128)S(1)} %bitcast.124), kind=kOutput, calls=%fused_computation.4 | convolution fusion | flops 152961024 | bytes 9601024 | tf_op jit(solution)/shard_map/dot_general | solution.py:12
  (55 shorter events, 0.8 us)
Async XLA Ops:
  0.6 84.4 %copy-start = (f32[768,32]{0,1:T(8,128)S(1)}, f32[768,32]{0,1:T(8,128)}, u32[]{:S(2)}) copy-start(f32[768,32]{0,1:T(8,128)} %param.19) | copy-start | bytes 294916
  0.7 4.1 %copy-start.2 = (f32[1,512,768]{2,1,0:T(8,128)S(1)}, f32[1,512,768]{2,1,0:T(8,128)}, u32[]{:S(2)}) copy-start(f32[1,512,768]{2,1,0:T(8,128)} %param.16) | copy-start | bytes 4718596
  3.7 1.1 copy-start.7
  6.6 1.9 %copy-start.3 = (f32[32,18,128]{2,1,0:T(8,128)S(1)}, f32[32,18,128]{2,1,0:T(8,128)}, u32[]{:S(2)}) copy-start(f32[32,18,128]{2,1,0:T(8,128)} %copy.53) | copy-start | bytes 884740
  68.2 16.0 %copy-start.8 = (f32[768,32]{0,1:T(8,128)S(1)}, f32[768,32]{0,1:T(8,128)}, u32[]{:S(2)}) copy-start(f32[768,32]{0,1:T(8,128)} %param.25) | copy-start | bytes 294916
  69.9 14.6 %copy-start.9 = (f32[2,32,32]{2,1,0:T(8,128)S(1)}, f32[2,32,32]{2,1,0:T(8,128)}, u32[]{:S(2)}) copy-start(f32[2,32,32]{2,1,0:T(8,128)} %param.26) | copy-start | bytes 24580
  84.2 1.4 copy-start.12
  121.5 15.7 %all-to-all-start.4 = ((f32[32,16,128]{2,1,0:T(8,128)}), f32[32,16,128]{2,1,0:T(8,128)S(1)}, u32[]{:S(2)}, u32[]{:S(2)}) async-start(f32[32,16,128]{2,1,0:T(8,128)} %pad.21), calls=%async_computation.4 | async-start | bytes 524288 | tf_op jit(solution)/shard_map/all_to_all | solution.py:22
  137.3 24.2 %copy-start.10 = (f32[480]{0:T(512)S(1)}, f32[480]{0:T(512)}, u32[]{:S(2)}) copy-start(f32[480]{0:T(512)} %param.29) | copy-start | bytes 5764
  137.3 24.2 %copy-start.11 = (f32[480]{0:T(512)S(1)}, f32[480]{0:T(512)}, u32[]{:S(2)}) copy-start(f32[480]{0:T(512)} %param.28) | copy-start | bytes 5764
  154.1 1.0 copy-start.4
  155.8 8.7 %copy-start.1 = (f32[512,768]{1,0:T(8,128)S(1)}, f32[512,768]{1,0:T(8,128)}, u32[]{:S(2)}) copy-start(f32[512,768]{1,0:T(8,128)} %param.18) | copy-start | bytes 4718596
  159.7 4.8 %copy-start.5 = (f32[512,32]{1,0:T(8,128)S(1)}, f32[512,32]{1,0:T(8,128)}, u32[]{:S(2)}) copy-start(f32[512,32]{1,0:T(8,128)} %reshape.105) | copy-start | bytes 196612
  159.7 4.8 %copy-start.6 = (f32[2,16,6,128]{3,2,1,0:T(8,128)S(1)}, f32[2,16,6,128]{3,2,1,0:T(8,128)}, u32[]{:S(2)}) copy-start(f32[2,16,6,128]{3,2,1,0:T(8,128)} %copy.62) | copy-start | bytes 294916

commit v2 on v1

v2 whole, which is shorter than its diff:
```python
import functools

import jax
import jax.numpy as jnp
from jax import lax
from jax.experimental import pallas as pl
from jax.experimental.pallas import tpu as pltpu
from jax.sharding import PartitionSpec as P

decay_rate = 0.9
step_rate = 0.01
LANES = 128
ROWS = 8
VMEM_LIMIT = 24 * 1024 * 1024


def dot(left, right, contract):
    return lax.dot_general(
        left,
        right,
        ((contract[0], contract[1]), ((), ())),
        precision=lax.Precision.HIGHEST,
        preferred_element_type=jnp.float32,
    )


def exchange(blocks, axis, groups=None):
    return lax.all_to_all(blocks, axis, 0, 0, axis_index_groups=groups)


def spread(block, axis):
    return exchange(jnp.broadcast_to(block[None], (lax.axis_size(axis),) + block.shape), axis)


def pack_kernel(gradient, error, rest, merged, sent):
    total = gradient[...].astype(jnp.float32) + error[...]
    merged[...] = total
    blocks = sent.shape[0]
    per = total.shape[0] // blocks
    cols = total.shape[1] // LANES
    for col in range(cols):
        piece = total[:, col * LANES : (col + 1) * LANES].reshape(blocks, per, LANES)
        sent[:, col * per : (col + 1) * per, :] = piece
    sent[:, cols * per :, :] = rest[...]


def pack(gradient, error, rest, steps):
    rows, width = gradient.shape
    blocks = rest.shape[0]
    height = rows // blocks * (width // LANES) + rest.shape[1]
    return pl.pallas_call(
        pack_kernel,
        grid=(steps,),
        in_specs=[
            pl.BlockSpec((rows // steps, width), lambda i: (i, 0)),
            pl.BlockSpec((rows // steps, width), lambda i: (i, 0)),
            pl.BlockSpec((blocks // steps, rest.shape[1], LANES), lambda i: (i, 0, 0)),
        ],
        out_specs=[
            pl.BlockSpec((rows // steps, width), lambda i: (i, 0)),
            pl.BlockSpec((blocks // steps, height, LANES), lambda i: (i, 0, 0)),
        ],
        out_shape=[
            jax.ShapeDtypeStruct((rows, width), jnp.float32),
            jax.ShapeDtypeStruct((blocks, height, LANES), jnp.float32),
        ],
        compiler_params=pltpu.CompilerParams(vmem_limit_bytes=VMEM_LIMIT),
        name="pack",
    )(gradient, error, rest)


def apply(approx, merged, moment, weight, residual, velocity, updated):
    residual[...] = merged - approx
    speed = decay_rate * moment + approx
    velocity[...] = speed
    updated[...] = weight - step_rate * speed


def finish_kernel(
    rank, tiles, every, warm, mt, vt, wt, gq, eq, vq, wq, rt_out, vt_out, ut_out, rq_out, vq_out, uq_out
):
    some = tiles.shape[0]
    tile = tiles[...].reshape(some * ROWS, LANES)
    width = warm.shape[1]
    halves = [
        dot(tile[:, h * rank : (h + 1) * rank], warm[:rank, :], ((1,), (0,))).reshape(some, 1, ROWS, width)
        for h in range(2)
    ]
    approx = jnp.concatenate(halves, axis=1).reshape(2 * some * ROWS, width)
    apply(approx, mt[...], vt[...], wt[...], rt_out, vt_out, ut_out)

    @pl.when(pl.program_id(0) == 0)
    def _():
        per = every.shape[0]
        for i in range(gq.shape[0] // per):
            part = pl.ds(i * per, per)
            basis = every[:, i, :][:, 2 * rank : 3 * rank]
            merged = gq[part, :].astype(jnp.float32) + eq[part, :]
            apply(
                dot(basis, warm[rank:, :], ((1,), (0,))),
                merged,
                vq[part, :],
                wq[part, :],
                rq_out.at[part, :],
                vq_out.at[part, :],
                uq_out.at[part, :],
            )


def finish(rank, steps, tiles, warm, mt, vt, wt, gq, eq, vq, wq):
    rows, width = mt.shape
    rows_query = vq.shape[0]
    moving = pl.BlockSpec((rows // steps, width), lambda i: (i, 0))
    fixed = pl.BlockSpec((rows_query, width), lambda i: (0, 0))
    return pl.pallas_call(
        functools.partial(finish_kernel, rank),
        grid=(steps,),
        in_specs=[
            pl.BlockSpec((tiles.shape[0] // steps, ROWS, LANES), lambda i: (i, 0, 0)),
            pl.BlockSpec(tiles.shape, lambda i: (0, 0, 0)),
            pl.BlockSpec(warm.shape, lambda i: (0, 0)),
            moving,
            moving,
            moving,
            fixed,
            fixed,
            fixed,
            fixed,
        ],
        out_specs=[moving] * 3 + [fixed] * 3,
        out_shape=[jax.ShapeDtypeStruct((rows, width), jnp.float32)] * 3
        + [jax.ShapeDtypeStruct((rows_query, width), jnp.float32)] * 3,
        compiler_params=pltpu.CompilerParams(vmem_limit_bytes=VMEM_LIMIT),
        name="finish",
    )(tiles, tiles, warm, mt, vt, wt, gq, eq, vq, wq)


def local(
    gradient_table,
    error_table,
    moment_table,
    weight_table,
    start_table,
    gram_table,
    gradient_query,
    error_query,
    moment_query,
    weight_query,
    start_query,
    gram_query,
    gradient_norms,
    moment_norms,
    weight_norms,
):
    replicas = lax.axis_size("replica")
    shards = lax.axis_size("shard")
    rows_table, width = moment_table.shape
    rows_query = moment_query.shape[0]
    rank = start_table.shape[1]
    cols = width // LANES
    per_table = rows_table // replicas
    per_query = rows_query // replicas
    entries = moment_norms.shape[0]
    per_norms = entries // replicas
    fours, eights = 4, replicas // 4
    across = [[eights * first + second for first in range(fours)] for second in range(eights)]
    along = [[eights * first + second for second in range(eights)] for first in range(fours)]

    n_table = per_table * cols
    n_query = per_query * cols
    filled = n_table + n_query
    height = -(-(filled + 1) // ROWS) * ROWS
    merged_query = gradient_query[0].astype(jnp.float32) + error_query[0]
    rest = merged_query.reshape(per_query, replicas, cols, LANES).transpose(1, 0, 2, 3)
    norms = gradient_norms[0].reshape(replicas, 1, per_norms)
    norms = jnp.pad(norms, ((0, 0), (0, height - filled - 1), (0, LANES - per_norms)))
    rest = jnp.concatenate([rest.reshape(replicas, n_query, LANES), norms], axis=1)
    merged_table, sent = pack(gradient_table[0], error_table[0], rest, fours)

    blocks = sent.reshape(fours, eights * height, LANES)
    blocks = jnp.sum(exchange(blocks, "replica", across), axis=0).reshape(eights, height, LANES)
    own = jnp.sum(exchange(blocks, "replica", along), axis=0)

    rows = spread(own, "shard")

    sum_table = rows[:, :n_table].reshape(shards, cols, per_table, LANES).transpose(0, 2, 1, 3)
    sum_table = sum_table.reshape(shards * per_table, width)
    sum_query = rows[:, n_table:filled].reshape(shards * per_query, width)

    tall = 16
    stack = 2 * rank // tall
    used = cols * stack

    def reduce_right(basis_table, basis_query):
        right = jnp.concatenate(
            [dot(basis_table, sum_table, ((0,), (0,))), dot(basis_query, sum_query, ((0,), (0,)))], axis=0
        )
        blocks = right.reshape(stack, tall, cols, LANES).transpose(2, 0, 1, 3).reshape(used, tall, LANES)
        blocks = jnp.pad(blocks, ((0, replicas - used), (0, 0), (0, 0)))
        return jnp.sum(exchange(blocks, "replica"), axis=0) / replicas

    def stacked(blocks):
        blocks = blocks[:used].reshape(cols, stack, tall, LANES).transpose(1, 2, 0, 3)
        return blocks.reshape(2 * rank, width)

    basis_table = dot(dot(sum_table, start_table, ((1,), (0,))) / replicas, gram_table[0], ((1,), (0,)))
    basis_query = dot(dot(sum_query, start_query, ((1,), (0,))) / replicas, gram_query[0], ((1,), (0,)))
    right = stacked(spread(reduce_right(basis_table, basis_query), "replica"))
    basis_table = dot(dot(sum_table, right[:rank], ((1,), (1,))) / replicas, gram_table[1], ((1,), (0,)))
    basis_query = dot(dot(sum_query, right[rank:], ((1,), (1,))) / replicas, gram_query[1], ((1,), (0,)))

    shard = lax.axis_index("shard")
    mine_table = lax.dynamic_slice_in_dim(basis_table, shard * per_table, per_table, 0)
    mine_query = lax.dynamic_slice_in_dim(basis_query, shard * per_query, per_query, 0)
    mine_query = jnp.pad(mine_query, ((0, ROWS - per_query), (0, 0)))
    mine_norms = jnp.pad(own[filled : filled + 1, :rank], ((0, ROWS - 1), (0, 0)))
    mine = jnp.concatenate([mine_table[:ROWS], mine_table[ROWS:], mine_query, mine_norms], axis=1)
    mine = jnp.concatenate([mine, reduce_right(basis_table, basis_query)], axis=0)
    final = spread(mine, "replica")

    tiles = final[:, :ROWS]
    warm = stacked(final[:, ROWS:])
    mean_norms = final[:, 0, 3 * rank : 3 * rank + per_norms].reshape(entries) / replicas
    velocity_norms = decay_rate * moment_norms + mean_norms
    updated_norms = weight_norms - step_rate * velocity_norms
    residual_table, velocity_table, updated_table, residual_query, velocity_query, updated_query = finish(
        rank,
        4,
        tiles,
        warm,
        merged_table,
        moment_table,
        weight_table,
        gradient_query[0],
        error_query[0],
        moment_query,
        weight_query,
    )
    return (
        residual_table[None],
        velocity_table,
        updated_table,
        warm[:rank].T,
        residual_query[None],
        velocity_query,
        updated_query,
        warm[rank:].T,
        velocity_norms,
        updated_norms,
    )


def solution(mesh):
    per_replica = P("replica", "shard", None)
    per_shard = P("shard", None)
    matrix = (per_replica, per_replica, per_shard, per_shard, P(), P())
    return jax.shard_map(
        local,
        mesh=mesh,
        in_specs=matrix + matrix + (P("replica", "shard"), P("shard"), P("shard")),
        out_specs=(per_replica, per_shard, per_shard, P()) * 2 + (P("shard"), P("shard")),
        check_vma=False,
    )
```

time: 170 us -> 157 us (0.924)
  matrix products: 11 us -> 3.38 us
  blocking collectives: 123 us -> 116 us
  Pallas kernels: 0 us -> 4.49 us
  local copies, waits for them, and re-layouts: 14.2 us -> 12.4 us
    dot_general x14 -> x12, matrix products: 11 us -> 3.38 us  [dot(): lax.dot_general(left, right, ((contract[0], contract[1]), ((), ())), prec...]
    all_to_all x5 -> x6, blocking collectives: 123 us -> 116 us  [exchange(): return lax.all_to_all(blocks, axis, 0, 0, axis_index_groups=groups)]
    unnamed x28 -> x32, local copies, waits for them, and re-layouts: 0.74 us -> 7.05 us
    pallas_call x0 -> x2, Pallas kernels: none -> 4.49 us  [the longest x1 4.21 us: finish(): pl.pallas_call(functools.partial(finish_kernel, rank), grid=(steps,), in_...]
    reshape x5 -> x4, local copies, waits for them, and re-layouts: 2.89 us -> 0.45 us  [the longest x1 0.18 us: local(): rest.reshape(replicas, n_query, LANES)]
    transpose x3 -> x1, local copies, waits for them, and re-layouts: 2.01 us -> 0.05 us  [local(): merged_query.reshape(per_query, replicas, cols, LANES).transpose(1, 0, 2, 3)]
    slice x8, local copies, waits for them, and re-layouts: 3.08 us -> 1.18 us  [the longest x1 0.91 us: local(): tiles = final[:, :ROWS]]
where the time goes in v2:
time: 157 us
  blocking collectives  116 us (74%)
  local copies, waits for them, and re-layouts  12.4 us (8%)
  waiting for transfers between devices  10.9 us (7%)
  starting transfers between devices  4.56 us (3%)
  Pallas kernels  4.49 us (3%)
  other arithmetic  4.21 us (3%)
  matrix products  3.38 us (2%)
    all_to_all x6, blocking collectives, exchange(): return lax.all_to_all(blocks, axis, 0, 0, axis_index_groups=groups)  116 us
    all_to_all x1, waiting for transfers between devices, exchange(): return lax.all_to_all(blocks, axis, 0, 0, axis_index_groups=groups)  10.9 us
    unnamed x32, local copies, waits for them, and re-layouts  7.05 us
    all_to_all x1, starting transfers between devices, exchange(): return lax.all_to_all(blocks, axis, 0, 0, axis_index_groups=groups)  4.56 us
    pallas_call x1, Pallas kernels, finish(): pl.pallas_call(functools.partial(finish_kernel, rank), grid=(steps,), in_...  4.21 us
    dot_general x12, matrix products, dot(): lax.dot_general(left, right, ((contract[0], contract[1]), ((), ())), prec...  3.38 us
  transfers between devices with their start and end apart: 1, of which 1 were waited for; matrix products, arithmetic and copies ran while one was open for 0% of the time, Pallas kernels for 0%

profile of v2, /device:TPU:32, one launch (start us, length us, event | category | flops | bytes accessed | tf_op | source)
XLA Modules:
  0.0 156.7 jit_solution(12851847425224866877)
XLA Ops:
  0.7 0.5 broadcast.66
  1.2 1.3 reduce.7
  2.5 0.1 reshape_squeeze.4
  2.6 1.0 convert_add_fusion
  3.8 0.2 copy.65
  4.0 1.0 copy-done.1
  5.1 0.2 copy-done.7
  5.3 0.3 pack.1
  5.6 1.1 copy-done.4
  6.7 29.0 %all_to_all.35 = f32[4,960,128]{2,1,0:T(8,128)S(1)} all-to-all(f32[4,960,128]{2,1,0:T(8,128)S(1)} %bitcast.88), channel_id=1, replica_groups={{0,64,128,192},{8,72,136,200},{16,80,144,208},{24,88,152,216},{32,96,16..., dimensions={0} | all-to-all | bytes 3932160 | tf_op jit(solution)/shard_map/all_to_all | solution.py:28
  35.7 0.1 reduce_sum.36
  35.9 22.7 %all_to_all.36 = f32[8,120,128]{2,1,0:T(8,128)S(1)} all-to-all(f32[8,120,128]{2,1,0:T(8,128)S(1)} %bitcast.100), channel_id=1, replica_groups={{0,8,16,24,32,40,48,56},{64,72,80,88,96,104,112,120},{128,136,144,152,1..., dimensions={0} | all-to-all | bytes 983040 | tf_op jit(solution)/shard_map/all_to_all | solution.py:28
  58.7 14.2 %all_to_all.37 = f32[8,120,128]{2,1,0:T(8,128)S(1)} all-to-all(f32[8,120,128]{2,1,0:T(8,128)S(1)} %broadcast_in_dim.10), channel_id=1, replica_groups=mesh['replica'=32,'shard'=8] {'shard'}, dimensions={0} | all-to-all | bytes 983040 | tf_op jit(solution)/shard_map/all_to_all | solution.py:28
  72.9 0.2 convolution_multiply_fusion.3
  73.2 0.1 fusion.19
  73.3 0.3 fusion.33
  73.6 0.1 copy.66
  73.8 0.5 convolution_multiply_fusion.1
  74.3 0.2 fusion.21
  74.5 0.4 fusion.3
  75.0 16.4 %all_to_all.38 = f32[32,16,128]{2,1,0:T(8,128)S(1)} all-to-all(f32[32,16,128]{2,1,0:T(8,128)S(1)} %pad.20), channel_id=1, replica_groups=mesh['replica'=32,'shard'=8] {'replica'}, dimensions={0} | all-to-all | bytes 524288 | tf_op jit(solution)/shard_map/all_to_all | solution.py:28
  91.5 15.8 %all_to_all.39 = f32[32,16,128]{2,1,0:T(8,128)S(1)} all-to-all(f32[32,16,128]{2,1,0:T(8,128)S(1)} %broadcast_in_dim.11), channel_id=1, replica_groups=mesh['replica'=32,'shard'=8] {'replica'}, dimensions={0} | all-to-all | bytes 524288 | tf_op jit(solution)/shard_map/all_to_all | solution.py:28
  107.5 0.5 convolution_multiply_fusion
  108.0 0.2 fusion.17
  108.2 0.4 fusion
  108.6 0.2 convolution_multiply_fusion.2
  108.8 0.2 fusion.15
  109.0 0.3 fusion.34
  109.4 0.7 pad.23
  110.1 4.6 %all-to-all-start.5 = ((f32[32,16,128]{2,1,0:T(8,128)}), f32[32,16,128]{2,1,0:T(8,128)S(1)}, u32[]{:S(2)}, u32[]{:S(2)}) async-start(f32[32,16,128]{2,1,0:T(8,128)} %pad.23), calls=%async_computation.5 | async-start | bytes 524288 | tf_op jit(solution)/shard_map/all_to_all | solution.py:28
  114.7 0.1 constant_dynamic-slice_fusion
  114.8 0.1 copy.70
  114.8 0.1 copy.71
  114.9 10.9 %all-to-all-done.5 = f32[32,16,128]{2,1,0:T(8,128)S(1)} async-done(((f32[32,16,128]{2,1,0:T(8,128)}), f32[32,16,128]{2,1,0:T(8,128)S(1)}, u32[]{:S(2)}, u32[]{:S(2)}) %all-to-all-start.5) | async-done | bytes 262176 | tf_op jit(solution)/shard_map/all_to_all | solution.py:28
  125.9 0.1 fusion.27
  126.0 17.4 %all_to_all.40 = f32[32,24,128]{2,1,0:T(8,128)S(1)} all-to-all(f32[32,24,128]{2,1,0:T(8,128)S(1)} %broadcast_in_dim.12), channel_id=1, replica_groups=mesh['replica'=32,'shard'=8] {'replica'}, dimensions={0} | all-to-all | bytes 786432 | tf_op jit(solution)/shard_map/all_to_all | solution.py:28
  143.4 0.7 copy-done.11
  144.2 0.1 fusion.14
  144.3 0.7 div.34
  145.0 1.0 slice.93
  146.0 0.1 copy.110
  146.2 0.7 bitcast_bitcast_fusion
  146.9 1.3 multiply_subtract_fusion
  148.2 0.9 slice.92.tiles.every
  149.2 1.4 copy-done.5
  150.6 1.0 copy-done.9
  151.5 1.0 copy-done.10
  152.5 4.2 %finish.1 = (f32[512,768]{1,0:T(8,128)}, f32[512,768]{1,0:T(8,128)}, f32[512,768]{1,0:T(8,128)}, f32[96,768]{1,0:T(8,128)}, f32[96,768]{1,0:T(8,128)}, /*index=5*/f32[96,768]{1,0:T(8,128)}) custom-call(f32[32,8,128]{2,1,0:T(8,128)S(1)} %slice.92.tiles.every, f32[32,8,128]{2,1,0:T(8,128)S(1)} %slice.92.tiles.every, f32[64,768]{1,0:T(8,128)S(1)} %bitcast.91, ...), custom_call_target="tpu_custom_call" | custom-call | tf_op jit(solution)/shard_map/finish/pallas_call | solution.py:115
  (52 shorter events, 0.9 us)
Async XLA Ops:
  0.6 73.1 %copy-start = (f32[768,32]{0,1:T(8,128)S(1)}, f32[768,32]{0,1:T(8,128)}, u32[]{:S(2)}) copy-start(f32[768,32]{0,1:T(8,128)} %param.19) | copy-start | bytes 294916
  3.7 1.4 copy-start.1
  3.7 1.6 %copy-start.7 = (bf16[1,512,768]{2,1,0:T(8,128)(2,1)S(1)}, bf16[1,512,768]{2,1,0:T(8,128)(2,1)}, u32[]{:S(2)}) copy-start(bf16[1,512,768]{2,1,0:T(8,128)(2,1)} %param.15) | copy-start | bytes 2359300
  5.6 1.1 copy-start.4
  35.9 37.1 %copy-start.12 = (f32[768,32]{0,1:T(8,128)S(1)}, f32[768,32]{0,1:T(8,128)}, u32[]{:S(2)}) copy-start(f32[768,32]{0,1:T(8,128)} %param.25) | copy-start | bytes 294916
  35.9 37.3 %copy-start.13 = (f32[2,32,32]{2,1,0:T(8,128)S(1)}, f32[2,32,32]{2,1,0:T(8,128)}, u32[]{:S(2)}) copy-start(f32[2,32,32]{2,1,0:T(8,128)} %param.26) | copy-start | bytes 24580
  72.9 1.4 copy-start.14
  110.1 15.7 %all-to-all-start.5 = ((f32[32,16,128]{2,1,0:T(8,128)}), f32[32,16,128]{2,1,0:T(8,128)S(1)}, u32[]{:S(2)}, u32[]{:S(2)}) async-start(f32[32,16,128]{2,1,0:T(8,128)} %pad.23), calls=%async_computation.5 | async-start | bytes 524288 | tf_op jit(solution)/shard_map/all_to_all | solution.py:28
  126.0 23.2 %copy-start.6 = (f32[1,96,768]{2,1,0:T(8,128)S(1)}, f32[1,96,768]{2,1,0:T(8,128)}, u32[]{:S(2)}) copy-start(f32[1,96,768]{2,1,0:T(8,128)} %param.22) | copy-start | bytes 884740
  126.0 23.1 %copy-start.2 = (f32[512,768]{1,0:T(8,128)S(1)}, f32[512,768]{1,0:T(8,128)}, u32[]{:S(2)}) copy-start(f32[512,768]{1,0:T(8,128)} %vt.1) | copy-start | bytes 4718596
  126.0 23.1 %copy-start.3 = (f32[512,768]{1,0:T(8,128)S(1)}, f32[512,768]{1,0:T(8,128)}, u32[]{:S(2)}) copy-start(f32[512,768]{1,0:T(8,128)} %wt.1) | copy-start | bytes 4718596
  143.4 0.7 copy-start.11
  145.0 4.1 %copy-start.8 = (bf16[1,96,768]{2,1,0:T(8,128)(2,1)S(1)}, bf16[1,96,768]{2,1,0:T(8,128)(2,1)}, u32[]{:S(2)}) copy-start(bf16[1,96,768]{2,1,0:T(8,128)(2,1)} %param.21) | copy-start | bytes 442372
  149.1 1.4 copy-start.5
  150.6 1.0 copy-start.9
  151.5 1.0 copy-start.10

commit v3 on v2

v3 whole, which is shorter than its diff:
```python
import functools

import jax
import jax.numpy as jnp
from jax import lax
from jax.experimental import pallas as pl
from jax.experimental.pallas import tpu as pltpu
from jax.sharding import PartitionSpec as P

decay_rate = 0.9
step_rate = 0.01
LANES = 128
ROWS = 8
VMEM_LIMIT = 24 * 1024 * 1024


def dot(left, right, contract):
    return lax.dot_general(
        left,
        right,
        ((contract[0], contract[1]), ((), ())),
        precision=lax.Precision.HIGHEST,
        preferred_element_type=jnp.float32,
    )


def exchange(blocks, axis, groups=None):
    return lax.all_to_all(blocks, axis, 0, 0, axis_index_groups=groups)


def spread(block, axis):
    return exchange(jnp.broadcast_to(block[None], (lax.axis_size(axis),) + block.shape), axis)


def pack_kernel(gradient, error, rest, sent):
    total = gradient[...].astype(jnp.float32) + error[...]
    blocks = sent.shape[0]
    per = total.shape[0] // blocks
    cols = total.shape[1] // LANES
    for col in range(cols):
        piece = total[:, col * LANES : (col + 1) * LANES].reshape(blocks, per, LANES)
        sent[:, col * per : (col + 1) * per, :] = piece
    sent[:, cols * per :, :] = rest[...]


def pack(gradient, error, rest, steps):
    rows, width = gradient.shape
    blocks = rest.shape[0]
    height = rows // blocks * (width // LANES) + rest.shape[1]
    return pl.pallas_call(
        pack_kernel,
        grid=(steps,),
        in_specs=[
            pl.BlockSpec((rows // steps, width), lambda i: (i, 0)),
            pl.BlockSpec((rows // steps, width), lambda i: (i, 0)),
            pl.BlockSpec((blocks // steps, rest.shape[1], LANES), lambda i: (i, 0, 0)),
        ],
        out_specs=pl.BlockSpec((blocks // steps, height, LANES), lambda i: (i, 0, 0)),
        out_shape=jax.ShapeDtypeStruct((blocks, height, LANES), jnp.float32),
        compiler_params=pltpu.CompilerParams(vmem_limit_bytes=VMEM_LIMIT),
        name="pack",
    )(gradient, error, rest)


def apply(approx, merged, moment, weight, residual, velocity, updated):
    residual[...] = merged - approx
    speed = decay_rate * moment + approx
    velocity[...] = speed
    updated[...] = weight - step_rate * speed


def finish_kernel(
    rank, core, mine, other, gt, et, vt, wt, gq, eq, vq, wq,
    rt_out, vt_out, ut_out, warm_table, rq_out, vq_out, uq_out, warm_query, tiles,
):
    step = pl.program_id(0)
    replicas = mine.shape[0]
    width = gt.shape[1]
    cols = width // LANES
    stack = rank // ROWS

    def pick(first, second):
        return jnp.where(core[0] == 0, first, second)

    def own(part):
        flat = part.reshape(replicas * ROWS, LANES)
        return pick(flat, pltpu.roll(flat, LANES // 2, 1)).reshape(replicas, ROWS, LANES)

    @pl.when(step == 0)
    def _():
        here, there = mine[...], other[...]
        for out, block in ((warm_table, pick(here, there)), (warm_query, pick(there, here))):
            for col in range(cols):
                for row in range(stack):
                    piece = block[col * stack + row, ROWS:, :]
                    out[row * ROWS : (row + 1) * ROWS, col * LANES : (col + 1) * LANES] = piece
        tiles[0] = own(pick(here[:, :ROWS, :], there[:, :ROWS, :]))
        tiles[1] = own(pick(there[:, :ROWS, :], here[:, :ROWS, :]))
        for i in range(gq.shape[0] // replicas):
            part = pl.ds(i * replicas, replicas)
            basis = tiles[1, :, i, :][:, :rank]
            merged = gq[part, :].astype(jnp.float32) + eq[part, :]
            apply(
                dot(basis, warm_query[...], ((1,), (0,))),
                merged,
                vq[part, :],
                wq[part, :],
                rq_out.at[part, :],
                vq_out.at[part, :],
                uq_out.at[part, :],
            )

    some = gt.shape[0] // (2 * ROWS)
    tile = tiles[0, pl.ds(pl.multiple_of(step * some, some), some)].reshape(some * ROWS, LANES)
    halves = [
        dot(tile[:, h * rank : (h + 1) * rank], warm_table[...], ((1,), (0,))).reshape(some, 1, ROWS, width)
        for h in range(2)
    ]
    approx = jnp.concatenate(halves, axis=1).reshape(2 * some * ROWS, width)
    merged = gt[...].astype(jnp.float32) + et[...]
    apply(approx, merged, vt[...], wt[...], rt_out, vt_out, ut_out)


def finish(rank, steps, core, mine, other, gt, et, vt, wt, gq, eq, vq, wq):
    rows, width = gt.shape
    rows_query = gq.shape[0]
    moving = pl.BlockSpec((rows // steps, width), lambda i: (i, 0))
    fixed = pl.BlockSpec((rows_query, width), lambda i: (0, 0))
    factor = pl.BlockSpec((rank, width), lambda i: (0, 0))
    whole = pl.BlockSpec(mine.shape, lambda i: (0, 0, 0))
    shape = functools.partial(jax.ShapeDtypeStruct, dtype=jnp.float32)
    return pl.pallas_call(
        functools.partial(finish_kernel, rank),
        grid=(steps,),
        in_specs=[pl.BlockSpec(memory_space=pltpu.SMEM), whole, whole] + [moving] * 4 + [fixed] * 4,
        out_specs=[moving] * 3 + [factor] + [fixed] * 3 + [factor],
        out_shape=[shape((rows, width))] * 3
        + [shape((rank, width))]
        + [shape((rows_query, width))] * 3
        + [shape((rank, width))],
        scratch_shapes=[pltpu.VMEM((2, mine.shape[0], ROWS, LANES), jnp.float32)],
        compiler_params=pltpu.CompilerParams(vmem_limit_bytes=VMEM_LIMIT),
        name="finish",
    )(core, mine, other, gt, et, vt, wt, gq, eq, vq, wq)


def local(
    gradient_table,
    error_table,
    moment_table,
    weight_table,
    start_table,
    gram_table,
    gradient_query,
    error_query,
    moment_query,
    weight_query,
    start_query,
    gram_query,
    gradient_norms,
    moment_norms,
    weight_norms,
):
    replicas = lax.axis_size("replica")
    shards = lax.axis_size("shard")
    rows_table, width = moment_table.shape
    rows_query = moment_query.shape[0]
    rank = start_table.shape[1]
    cols = width // LANES
    per_table = rows_table // replicas
    per_query = rows_query // replicas
    entries = moment_norms.shape[0]
    fours, eights = 4, replicas // 4
    across = [[eights * first + second for first in range(fours)] for second in range(eights)]
    along = [[eights * first + second for second in range(eights)] for first in range(fours)]

    n_table = per_table * cols
    n_query = per_query * cols
    n_norms = -(-entries // LANES)
    filled = n_table + n_query
    height = -(-(filled + n_norms) // ROWS) * ROWS
    merged_query = gradient_query[0].astype(jnp.float32) + error_query[0]
    rest = merged_query.reshape(per_query, replicas, cols, LANES).transpose(1, 0, 2, 3)
    norms = jnp.pad(gradient_norms, ((0, 0), (0, n_norms * LANES - entries))).reshape(1, n_norms, LANES)
    norms = jnp.broadcast_to(norms, (replicas, n_norms, LANES))
    rest = jnp.concatenate([rest.reshape(replicas, n_query, LANES), norms], axis=1)
    rest = jnp.pad(rest, ((0, 0), (0, height - filled - n_norms), (0, 0)))
    sent = pack(gradient_table[0], error_table[0], rest, fours)

    blocks = sent.reshape(fours, eights * height, LANES)
    blocks = jnp.sum(exchange(blocks, "replica", across), axis=0).reshape(eights, height, LANES)
    own = jnp.sum(exchange(blocks, "replica", along), axis=0)

    mean_norms = own[filled : filled + n_norms].reshape(n_norms * LANES)[:entries] / replicas
    velocity_norms = decay_rate * moment_norms + mean_norms
    updated_norms = weight_norms - step_rate * velocity_norms

    shard = lax.axis_index("shard")
    core = shard % 2
    query = own[n_table:filled].reshape(per_query, cols, LANES).transpose(1, 0, 2)
    query = jnp.pad(query, ((0, 0), (0, per_table - per_query), (0, 0))).reshape(n_table, LANES)
    both = jnp.stack([own[:n_table], query])
    both = jnp.broadcast_to(both[None], (shards // 2, 2, n_table, LANES)).reshape(shards, n_table, LANES)
    total = exchange(both, "shard").reshape(shards, cols, per_table, LANES).transpose(0, 2, 1, 3)
    total = total.reshape(shards * per_table, width)
    start = jnp.where(core == 0, start_table, start_query)
    gram = jnp.where(core == 0, gram_table, gram_query)

    stack = rank // ROWS
    used = cols * stack

    def reduce_right(basis):
        blocks = dot(basis, total, ((0,), (0,))).reshape(stack, ROWS, cols, LANES)
        blocks = blocks.transpose(2, 0, 1, 3).reshape(used, ROWS, LANES)
        blocks = jnp.pad(blocks, ((0, replicas - used), (0, 0), (0, 0)))
        return jnp.sum(exchange(blocks, "replica"), axis=0) / replicas

    basis = dot(dot(total, start, ((1,), (0,))) / replicas, gram[0], ((1,), (0,)))
    right = spread(reduce_right(basis), "replica")[:used]
    right = right.reshape(cols, stack, ROWS, LANES).transpose(1, 2, 0, 3).reshape(rank, width)
    basis = dot(dot(total, right, ((1,), (1,))) / replicas, gram[1], ((1,), (0,)))

    chip = lax.dynamic_slice_in_dim(basis, shard // 2 * (2 * per_table), 2 * per_table, 0)
    chip = jnp.concatenate([chip[i * ROWS : (i + 1) * ROWS] for i in range(2 * per_table // ROWS)], axis=1)
    mine = spread(jnp.concatenate([chip, reduce_right(basis)], axis=0), "replica")
    other = lax.ppermute(mine, "shard", [(i, i ^ 1) for i in range(shards)])
    (
        residual_table,
        velocity_table,
        updated_table,
        warm_table,
        residual_query,
        velocity_query,
        updated_query,
        warm_query,
    ) = finish(
        rank,
        4,
        core.reshape(1),
        mine,
        other,
        gradient_table[0],
        error_table[0],
        moment_table,
        weight_table,
        gradient_query[0],
        error_query[0],
        moment_query,
        weight_query,
    )
    return (
        residual_table[None],
        velocity_table,
        updated_table,
        warm_table.T,
        residual_query[None],
        velocity_query,
        updated_query,
        warm_query.T,
        velocity_norms,
        updated_norms,
    )


def solution(mesh):
    per_replica = P("replica", "shard", None)
    per_shard = P("shard", None)
    matrix = (per_replica, per_replica, per_shard, per_shard, P(), P())
    return jax.shard_map(
        local,
        mesh=mesh,
        in_specs=matrix + matrix + (P("replica", "shard"), P("shard"), P("shard")),
        out_specs=(per_replica, per_shard, per_shard, P()) * 2 + (P("shard"), P("shard")),
        check_vma=False,
    )
```

time: 157 us -> 147 us (0.936); the launches traced: 157 us -> 145 us
  blocking collectives: 116 us -> 94.7 us
  starting transfers between devices: 4.56 us -> 8.96 us
  waiting for transfers between devices: 10.9 us -> 15.3 us
    all_to_all x6 -> x5, blocking collectives: 116 us -> 94.7 us  [exchange(): return lax.all_to_all(blocks, axis, 0, 0, axis_index_groups=groups)]
    all_to_all x1 -> x2, waiting for transfers between devices: 10.9 us -> 15.3 us  [exchange(): return lax.all_to_all(blocks, axis, 0, 0, axis_index_groups=groups)]
    all_to_all x1 -> x2, starting transfers between devices: 4.56 us -> 8.95 us  [exchange(): return lax.all_to_all(blocks, axis, 0, 0, axis_index_groups=groups)]
    unnamed x32 -> x36, local copies, waits for them, and re-layouts: 7.05 us -> 5.15 us
    dot_general x12 -> x6, matrix products: 3.38 us -> 4.33 us  [dot(): lax.dot_general(left, right, ((contract[0], contract[1]), ((), ())), prec...]
  transfers between devices with their start and end apart: 1 -> 3, of which waited for: 1 -> 2; matrix products, arithmetic and copies ran while one was open for 0% -> 4% of each run, Pallas kernels for 0% -> 0%
where the time goes in v3:
time: 147 us; the launch traced here: 145 us
  blocking collectives  94.7 us (64%)
  waiting for transfers between devices  15.3 us (10%)
  local copies, waits for them, and re-layouts  12.1 us (8%)
  starting transfers between devices  8.96 us (6%)
  Pallas kernels  4.39 us (3%)
  matrix products  4.33 us (3%)
  other arithmetic  4.27 us (3%)
    all_to_all x5, blocking collectives, exchange(): return lax.all_to_all(blocks, axis, 0, 0, axis_index_groups=groups)  94.7 us
    all_to_all x2, waiting for transfers between devices, exchange(): return lax.all_to_all(blocks, axis, 0, 0, axis_index_groups=groups)  15.3 us
    all_to_all x2, starting transfers between devices, exchange(): return lax.all_to_all(blocks, axis, 0, 0, axis_index_groups=groups)  8.95 us
    unnamed x36, local copies, waits for them, and re-layouts  5.15 us
    dot_general x6, matrix products, dot(): lax.dot_general(left, right, ((contract[0], contract[1]), ((), ())), prec...  4.33 us
    pallas_call x1, Pallas kernels, finish(): pl.pallas_call(functools.partial(finish_kernel, rank), grid=(steps,), in_...  4.18 us
    slice x5, local copies, waits for them, and re-layouts, local(): chip[i * ROWS:(i + 1) * ROWS]  3.12 us
  transfers between devices with their start and end apart: 3, of which 2 were waited for; matrix products, arithmetic and copies ran while one was open for 4% of the time, Pallas kernels for 0%

profile of v3, /device:TPU:32, one launch (start us, length us, event | category | flops | bytes accessed | tf_op | source)
XLA Modules:
  0.0 145.1 jit_solution(14844798174384907724)
XLA Ops:
  0.7 1.0 convert_add_fusion
  1.7 0.0 copy-start
  1.7 0.0 copy-start.1
  1.8 0.1 copy.66
  1.8 0.2 copy.67
  2.1 1.0 copy-done
  3.1 0.2 copy-done.1
  3.3 0.2 pack.1
  3.5 29.1 %all_to_all.35 = f32[4,960,128]{2,1,0:T(8,128)} all-to-all(f32[4,960,128]{2,1,0:T(8,128)S(1)} %bitcast.81), channel_id=1, replica_groups={{0,64,128,192},{8,72,136,200},{16,80,144,208},{24,88,152,216},{32,96,16..., dimensions={0} | all-to-all | bytes 3932160 | tf_op jit(solution)/shard_map/all_to_all | solution.py:28
  32.6 1.7 %reduce_sum.36 = f32[960,128]{1,0:T(8,128)S(1)} reduce(f32[4,960,128]{2,1,0:T(8,128)} %all_to_all.35, f32[]{:T(128)} %constant.42.clone.1), dimensions={0}, to_apply=%region_0.1 | reduce | flops 368640 | bytes 2457604 | tf_op jit(solution)/shard_map/reduce_sum | solution.py:191
  34.3 0.0 copy-start.13
  34.4 0.0 copy-start.14
  34.4 22.6 %all_to_all.36 = f32[8,120,128]{2,1,0:T(8,128)S(1)} all-to-all(f32[8,120,128]{2,1,0:T(8,128)S(1)} %bitcast.93), channel_id=1, replica_groups={{0,8,16,24,32,40,48,56},{64,72,80,88,96,104,112,120},{128,136,144,152,1..., dimensions={0} | all-to-all | bytes 983040 | tf_op jit(solution)/shard_map/all_to_all | solution.py:28
  57.0 0.0 copy-start.10
  57.1 0.8 broadcast_in_dim.16
  57.8 4.5 %all-to-all-start.2 = ((f32[8,96,128]{2,1,0:T(8,128)}), f32[8,96,128]{2,1,0:T(8,128)S(1)}, u32[]{:S(2)}, u32[]{:S(2)}) async-start(f32[8,96,128]{2,1,0:T(8,128)} %bitcast.11), calls=%async_computation.2 | async-start | bytes 786432 | tf_op jit(solution)/shard_map/all_to_all | solution.py:28
  62.3 0.0 copy-start.12
  62.3 0.1 copy.70
  62.4 0.1 copy.71
  62.5 8.7 %all-to-all-done.2 = f32[8,96,128]{2,1,0:T(8,128)S(1)} async-done(((f32[8,96,128]{2,1,0:T(8,128)}), f32[8,96,128]{2,1,0:T(8,128)S(1)}, u32[]{:S(2)}, u32[]{:S(2)}) %all-to-all-start.2) | async-done | bytes 393248 | tf_op jit(solution)/shard_map/all_to_all | solution.py:28
  71.2 0.1 copy.69
  71.3 0.0 copy-start.8
  71.4 0.9 copy.97
  72.3 1.1 copy.72
  73.5 0.0 copy-start.9
  73.5 0.5 fusion
  74.0 0.1 convolution_bitcast_fusion.2
  74.1 0.5 convolution_bitcast_fusion.1
  74.6 13.9 %all_to_all.37 = f32[32,8,128]{2,1,0:T(8,128)S(1)} all-to-all(f32[32,8,128]{2,1,0:T(8,128)S(1)} %pad.22), channel_id=1, replica_groups=mesh['replica'=32,'shard'=8] {'replica'}, dimensions={0} | all-to-all | bytes 262144 | tf_op jit(solution)/shard_map/all_to_all | solution.py:28
  88.6 13.9 %all_to_all.38 = f32[32,8,128]{2,1,0:T(8,128)S(1)} all-to-all(f32[32,8,128]{2,1,0:T(8,128)S(1)} %broadcast_in_dim.34), channel_id=1, replica_groups=mesh['replica'=32,'shard'=8] {'replica'}, dimensions={0} | all-to-all | bytes 262144 | tf_op jit(solution)/shard_map/all_to_all | solution.py:28
  102.5 1.6 %convolution_multiply_fusion = f32[128,32]{0,1:T(8,128)S(1)} fusion(f32[16,8,6,128]{3,2,1,0:T(8,128)} %bitcast.90, f32[4,8,6,128]{3,1,0,2:T(8,128)S(1)} %bitcast.100), kind=kOutput, calls=%fused_computation.3 | convolution fusion | flops 37752832 | bytes 507904 | tf_op jit(solution)/shard_map/dot_general | solution.py:18
  104.1 0.1 fusion.9
  104.2 1.5 %convolution_bitcast_fusion = f32[6,4,8,128]{3,2,0,1:T(8,128)S(1)} fusion(f32[6,128,128,1]{2,1,0,3:T(8,128)} %bitcast.92, f32[128,32]{0,1:T(8,128)S(1)} %fusion.9), kind=kOutput, calls=%fused_computation | convolution fusion | flops 37748736 | bytes 507904 | tf_op jit(solution)/shard_map/dot_general | solution.py:18
  105.7 0.7 pad.23
  106.4 4.5 %all-to-all-start.5 = ((f32[32,8,128]{2,1,0:T(8,128)}), f32[32,8,128]{2,1,0:T(8,128)S(1)}, u32[]{:S(2)}, u32[]{:S(2)}) async-start(f32[32,8,128]{2,1,0:T(8,128)} %pad.23), calls=%async_computation.5 | async-start | bytes 262144 | tf_op jit(solution)/shard_map/all_to_all | solution.py:28
  110.9 0.7 constant_dynamic-slice_fusion.2
  111.6 0.8 copy.75
  112.4 0.8 copy.77
  113.2 0.8 copy.76
  114.0 0.1 copy.78
  114.0 6.6 %all-to-all-done.5 = f32[32,8,128]{2,1,0:T(8,128)S(1)} async-done(((f32[32,8,128]{2,1,0:T(8,128)}), f32[32,8,128]{2,1,0:T(8,128)S(1)}, u32[]{:S(2)}, u32[]{:S(2)}) %all-to-all-start.5) | async-done | bytes 131104 | tf_op jit(solution)/shard_map/all_to_all | solution.py:28
  120.7 0.1 pad_maximum_fusion.1
  120.8 15.2 %all_to_all.39.mine = f32[32,16,128]{2,1,0:T(8,128)S(1)} all-to-all(f32[32,16,128]{2,1,0:T(8,128)S(1)} %broadcast_in_dim.35), channel_id=1, replica_groups=mesh['replica'=32,'shard'=8] {'replica'}, dimensions={0} | all-to-all | bytes 524288 | tf_op jit(solution)/shard_map/all_to_all | solution.py:28
  136.0 0.7 slice_bitcast_fusion.5
  136.7 1.3 multiply_subtract_fusion
  138.1 1.4 copy-done.2
  139.5 1.4 copy-done.3
  140.9 4.2 %finish.1 = (f32[512,768]{1,0:T(8,128)}, f32[512,768]{1,0:T(8,128)}, f32[512,768]{1,0:T(8,128)}, f32[32,768]{1,0:T(8,128)}, f32[96,768]{1,0:T(8,128)}, /*index=5...) custom-call(s32[1]{0:T(128)} %bitcast.core, f32[32,16,128]{2,1,0:T(8,128)S(1)} %all_to_all.39.mine, ...), custom_call_target="tpu_custom_call" | custom-call | tf_op jit(solution)/shard_map/finish/pallas_call | solution.py:132
  (44 shorter events, 0.4 us)
Async XLA Ops:
  0.6 1.4 copy-start.15
  1.7 1.4 copy-start
  1.7 1.6 %copy-start.1 = (bf16[1,512,768]{2,1,0:T(8,128)(2,1)S(1)}, bf16[1,512,768]{2,1,0:T(8,128)(2,1)}, u32[]{:S(2)}) copy-start(bf16[1,512,768]{2,1,0:T(8,128)(2,1)} %param.15) | copy-start | bytes 2359300
  34.3 28.0 %copy-start.13 = (f32[2,32,32]{2,1,0:T(8,128)S(1)}, f32[2,32,32]{2,1,0:T(8,128)}, u32[]{:S(2)}) copy-start(f32[2,32,32]{2,1,0:T(8,128)} %param.20) | copy-start | bytes 24580
  34.4 28.1 %copy-start.14 = (f32[2,32,32]{2,1,0:T(8,128)S(1)}, f32[2,32,32]{2,1,0:T(8,128)}, u32[]{:S(2)}) copy-start(f32[2,32,32]{2,1,0:T(8,128)} %param.26) | copy-start | bytes 24580
  57.0 0.9 copy-start.10
  57.8 13.4 %all-to-all-start.2 = ((f32[8,96,128]{2,1,0:T(8,128)}), f32[8,96,128]{2,1,0:T(8,128)S(1)}, u32[]{:S(2)}, u32[]{:S(2)}) async-start(f32[8,96,128]{2,1,0:T(8,128)} %bitcast.11), calls=%async_computation.2 | async-start | bytes 786432 | tf_op jit(solution)/shard_map/all_to_all | solution.py:28
  62.3 11.1 %copy-start.11 = (f32[768,32]{0,1:T(8,128)S(1)}, f32[768,32]{0,1:T(8,128)}, u32[]{:S(2)}) copy-start(f32[768,32]{0,1:T(8,128)} %param.19) | copy-start | bytes 294916
  62.3 11.2 %copy-start.12 = (f32[768,32]{0,1:T(8,128)S(1)}, f32[768,32]{0,1:T(8,128)}, u32[]{:S(2)}) copy-start(f32[768,32]{0,1:T(8,128)} %param.25) | copy-start | bytes 294916
  71.3 3.3 %copy-start.8 = (f32[8,16,6,128]{3,2,1,0:T(8,128)}, f32[8,16,6,128]{3,2,1,0:T(8,128)S(1)}, u32[]{:S(2)}) copy-start(f32[8,16,6,128]{3,2,1,0:T(8,128)S(1)} %copy.69) | copy-start | bytes 1179652
  73.5 15.1 %copy-start.9 = (f32[768,128]{1,0:T(8,128)}, f32[768,128]{1,0:T(8,128)S(1)}, u32[]{:S(2)}) copy-start(f32[768,128]{1,0:T(8,128)S(1)} %copy.72) | copy-start | bytes 1179652
  102.4 35.6 %copy-start.4 = (f32[1,96,768]{2,1,0:T(8,128)S(1)}, f32[1,96,768]{2,1,0:T(8,128)}, u32[]{:S(2)}) copy-start(f32[1,96,768]{2,1,0:T(8,128)} %param.22) | copy-start | bytes 884740
  102.4 35.6 %copy-start.5 = (bf16[1,96,768]{2,1,0:T(8,128)(2,1)S(1)}, bf16[1,96,768]{2,1,0:T(8,128)(2,1)}, u32[]{:S(2)}) copy-start(bf16[1,96,768]{2,1,0:T(8,128)(2,1)} %param.21) | copy-start | bytes 442372
  102.4 35.6 %copy-start.6 = (f32[96,768]{1,0:T(8,128)S(1)}, f32[96,768]{1,0:T(8,128)}, u32[]{:S(2)}) copy-start(f32[96,768]{1,0:T(8,128)} %vq.1) | copy-start | bytes 884740
  102.4 35.6 %copy-start.7 = (f32[96,768]{1,0:T(8,128)S(1)}, f32[96,768]{1,0:T(8,128)}, u32[]{:S(2)}) copy-start(f32[96,768]{1,0:T(8,128)} %wq.1) | copy-start | bytes 884740
  106.4 14.3 %all-to-all-start.5 = ((f32[32,8,128]{2,1,0:T(8,128)}), f32[32,8,128]{2,1,0:T(8,128)S(1)}, u32[]{:S(2)}, u32[]{:S(2)}) async-start(f32[32,8,128]{2,1,0:T(8,128)} %pad.23), calls=%async_computation.5 | async-start | bytes 262144 | tf_op jit(solution)/shard_map/all_to_all | solution.py:28
  136.0 2.0 %collective-permute-start = (f32[32,16,128]{2,1,0:T(8,128)S(1)}, f32[32,16,128]{2,1,0:T(8,128)S(1)}, u32[]{:S(2)}, u32[]{:S(2)}) collective-permute-start(f32[32,16,128]{2,1,0:T(8,128)S(1)} %all_to_all.39.mine), channel_id=1, source_target_pairs={{0,1},{1,0},{2,3},{3,2},{4,5},{5,4},{6,7},{7,6},{8,9},{9,8},{10,11... | collective-permute-start | bytes 786440 | tf_op jit(solution)/shard_map/ppermute | solution.py:226
  138.1 1.4 copy-start.2
  139.5 1.4 copy-start.3

commit v4 on v3

--- a/solution.py
+++ b/solution.py
@@ -12,6 +12,7 @@
 LANES = 128
 ROWS = 8
 VMEM_LIMIT = 24 * 1024 * 1024
+VMEM_ALL = 63 * 1024 * 1024
 
 
 def dot(left, right, contract):
@@ -139,7 +140,7 @@
         + [shape((rows_query, width))] * 3
         + [shape((rank, width))],
         scratch_shapes=[pltpu.VMEM((2, mine.shape[0], ROWS, LANES), jnp.float32)],
-        compiler_params=pltpu.CompilerParams(vmem_limit_bytes=VMEM_LIMIT),
+        compiler_params=pltpu.CompilerParams(vmem_limit_bytes=VMEM_ALL),
         name="finish",
     )(core, mine, other, gt, et, vt, wt, gq, eq, vq, wq)
 
@@ -201,10 +202,13 @@
     query = jnp.pad(query, ((0, 0), (0, per_table - per_query), (0, 0))).reshape(n_table, LANES)
     both = jnp.stack([own[:n_table], query])
     both = jnp.broadcast_to(both[None], (shards // 2, 2, n_table, LANES)).reshape(shards, n_table, LANES)
-    total = exchange(both, "shard").reshape(shards, cols, per_table, LANES).transpose(0, 2, 1, 3)
-    total = total.reshape(shards * per_table, width)
     start = jnp.where(core == 0, start_table, start_query)
     gram = jnp.where(core == 0, gram_table, gram_query)
+    total, start, gram, velocity_norms, updated_norms = lax.optimization_barrier(
+        (exchange(both, "shard"), start, gram, velocity_norms, updated_norms)
+    )
+    total = total.reshape(shards, cols, per_table, LANES).transpose(0, 2, 1, 3)
+    total = total.reshape(shards * per_table, width)
 
     stack = rank // ROWS
     used = cols * stack

time: 147 us -> 142 us (0.966)
  blocking collectives: 94.7 us -> 72 us
  waiting for transfers between devices: 15.3 us -> 33.2 us
  starting transfers between devices: 8.96 us -> 17.5 us
  local copies, waits for them, and re-layouts: 12.1 us -> 4.6 us
  Pallas kernels: 4.39 us -> 7.54 us
  matrix products: 4.33 us -> 2.24 us
    all_to_all x5 -> x4, blocking collectives: 94.7 us -> 72 us  [exchange(): return lax.all_to_all(blocks, axis, 0, 0, axis_index_groups=groups)]
    all_to_all x2 -> x3, waiting for transfers between devices: 15.3 us -> 31.7 us  [exchange(): return lax.all_to_all(blocks, axis, 0, 0, axis_index_groups=groups)]
    all_to_all x2 -> x3, starting transfers between devices: 8.95 us -> 17.5 us  [exchange(): return lax.all_to_all(blocks, axis, 0, 0, axis_index_groups=groups)]
    pallas_call x1, Pallas kernels: 4.18 us -> 7.33 us  [finish(): pl.pallas_call(functools.partial(finish_kernel, rank), grid=(steps,), in_...]
    unnamed x36 -> x26, local copies, waits for them, and re-layouts: 5.15 us -> 2.15 us
    slice x5, local copies, waits for them, and re-layouts: 3.12 us -> 0.34 us  [local(): chip[i * ROWS:(i + 1) * ROWS]]
    dot_general x6, matrix products: 4.33 us -> 2.24 us  [dot(): lax.dot_general(left, right, ((contract[0], contract[1]), ((), ())), prec...]
    ppermute x1, waiting for transfers between devices: 0.01 us -> 1.53 us  [local(): other = lax.ppermute(mine, 'shard', [(i, i ^ 1) for i in range(shards)])]
  transfers between devices with their start and end apart: 3 -> 4, of which waited for: 2 -> 4; matrix products, arithmetic and copies ran while one was open for 4% -> 1% of each run, Pallas kernels for 0% -> 0%
where the time goes in v4:
time: 142 us; the launch traced here: 141 us
  blocking collectives  72 us (51%)
  waiting for transfers between devices  33.2 us (23%)
  starting transfers between devices  17.5 us (12%)
  Pallas kernels  7.54 us (5%)
  local copies, waits for them, and re-layouts  4.6 us (3%)
  other arithmetic  2.8 us (2%)
  matrix products  2.24 us (2%)
    all_to_all x4, blocking collectives, exchange(): return lax.all_to_all(blocks, axis, 0, 0, axis_index_groups=groups)  72 us
    all_to_all x3, waiting for transfers between devices, exchange(): return lax.all_to_all(blocks, axis, 0, 0, axis_index_groups=groups)  31.7 us
    all_to_all x3, starting transfers between devices, exchange(): return lax.all_to_all(blocks, axis, 0, 0, axis_index_groups=groups)  17.5 us
    pallas_call x1, Pallas kernels, finish(): pl.pallas_call(functools.partial(finish_kernel, rank), grid=(steps,), in_...  7.33 us
  transfers between devices with their start and end apart: 4, of which 4 were waited for; matrix products, arithmetic and copies ran while one was open for 1% of the time, Pallas kernels for 0%

profile of v4, /device:TPU:32, one launch (start us, length us, event | category | flops | bytes accessed | tf_op | source)
XLA Modules:
  0.0 140.9 jit_solution(9114660829925694869)
XLA Ops:
  0.6 0.0 copy-start.10
  0.7 1.0 convert_add_fusion
  1.7 0.0 copy-start
  1.7 0.0 copy-start.1
  1.8 0.1 copy.67
  1.8 0.2 copy.68
  2.0 0.0 copy-done.10
  2.1 1.0 copy-done
  3.1 0.2 copy-done.1
  3.3 0.2 pack.1
  3.5 29.0 %all_to_all.35 = f32[4,960,128]{2,1,0:T(8,128)S(1)} all-to-all(f32[4,960,128]{2,1,0:T(8,128)S(1)} %bitcast.82), channel_id=1, replica_groups={{0,64,128,192},{8,72,136,200},{16,80,144,208},{24,88,152,216},{32,96,16..., dimensions={0} | all-to-all | bytes 3932160 | tf_op jit(solution)/shard_map/all_to_all | solution.py:29
  32.5 0.9 reduce_sum.36
  33.5 8.6 %all-to-all-start.1 = ((f32[8,120,128]{2,1,0:T(8,128)}), f32[8,120,128]{2,1,0:T(8,128)S(1)}, u32[]{:S(2)}, u32[]{:S(2)}) async-start(f32[8,120,128]{2,1,0:T(8,128)} %bitcast.7), calls=%async_computation.1 | async-start | bytes 983040 | tf_op jit(solution)/shard_map/all_to_all | solution.py:29
  42.0 0.1 copy.70
  42.1 0.1 copy.71
  42.2 0.0 copy-done.4
  42.2 0.0 copy-done.5
  42.2 14.0 %all-to-all-done.1 = f32[8,120,128]{2,1,0:T(8,128)S(1)} async-done(((f32[8,120,128]{2,1,0:T(8,128)}), f32[8,120,128]{2,1,0:T(8,128)S(1)}, u32[]{:S(2)}, u32[]{:S(2)}) %all-to-all-start.1) | async-done | bytes 491552 | tf_op jit(solution)/shard_map/all_to_all | solution.py:29
  56.3 0.8 broadcast_in_dim.16
  57.1 4.5 %all-to-all-start.2 = ((f32[8,96,128]{2,1,0:T(8,128)}), f32[8,96,128]{2,1,0:T(8,128)S(1)}, u32[]{:S(2)}, u32[]{:S(2)}) async-start(f32[8,96,128]{2,1,0:T(8,128)} %bitcast.11), calls=%async_computation.2 | async-start | bytes 786432 | tf_op jit(solution)/shard_map/all_to_all | solution.py:29
  61.6 0.6 multiply_subtract_fusion
  62.2 8.3 %all-to-all-done.2 = f32[8,96,128]{2,1,0:T(8,128)S(1)} async-done(((f32[8,96,128]{2,1,0:T(8,128)}), f32[8,96,128]{2,1,0:T(8,128)S(1)}, u32[]{:S(2)}, u32[]{:S(2)}) %all-to-all-start.2) | async-done | bytes 393248 | tf_op jit(solution)/shard_map/all_to_all | solution.py:29
  70.5 0.1 copy.72
  70.6 0.1 copy.98
  70.7 0.5 fusion
  71.2 0.2 copy.73
  71.4 0.1 convolution_bitcast_fusion.2
  71.5 0.5 convolution_bitcast_fusion.1
  72.0 13.9 %all_to_all.36 = f32[32,8,128]{2,1,0:T(8,128)S(1)} all-to-all(f32[32,8,128]{2,1,0:T(8,128)S(1)} %pad.22), channel_id=1, replica_groups=mesh['replica'=32,'shard'=8] {'replica'}, dimensions={0} | all-to-all | bytes 262144 | tf_op jit(solution)/shard_map/all_to_all | solution.py:29
  86.0 13.9 %all_to_all.37 = f32[32,8,128]{2,1,0:T(8,128)S(1)} all-to-all(f32[32,8,128]{2,1,0:T(8,128)S(1)} %broadcast_in_dim.34), channel_id=1, replica_groups=mesh['replica'=32,'shard'=8] {'replica'}, dimensions={0} | all-to-all | bytes 262144 | tf_op jit(solution)/shard_map/all_to_all | solution.py:29
  99.8 0.5 convolution_multiply_fusion
  100.3 0.1 fusion.9
  100.5 0.5 convolution_bitcast_fusion
  101.0 0.7 pad.23
  101.6 4.5 %all-to-all-start.5 = ((f32[32,8,128]{2,1,0:T(8,128)}), f32[32,8,128]{2,1,0:T(8,128)S(1)}, u32[]{:S(2)}, u32[]{:S(2)}) async-start(f32[32,8,128]{2,1,0:T(8,128)} %pad.23), calls=%async_computation.5 | async-start | bytes 262144 | tf_op jit(solution)/shard_map/all_to_all | solution.py:29
  106.2 0.1 constant_dynamic-slice_fusion.2
  106.2 0.1 copy.76
  106.3 0.1 copy.78
  106.4 0.1 copy.77
  106.4 0.1 copy.79
  106.5 9.4 %all-to-all-done.5 = f32[32,8,128]{2,1,0:T(8,128)S(1)} async-done(((f32[32,8,128]{2,1,0:T(8,128)}), f32[32,8,128]{2,1,0:T(8,128)S(1)}, u32[]{:S(2)}, u32[]{:S(2)}) %all-to-all-start.5) | async-done | bytes 131104 | tf_op jit(solution)/shard_map/all_to_all | solution.py:29
  116.0 0.1 pad_maximum_fusion.1
  116.1 15.2 %all_to_all.38.mine = f32[32,16,128]{2,1,0:T(8,128)S(1)} all-to-all(f32[32,16,128]{2,1,0:T(8,128)S(1)} %broadcast_in_dim.35), channel_id=1, replica_groups=mesh['replica'=32,'shard'=8] {'replica'}, dimensions={0} | all-to-all | bytes 524288 | tf_op jit(solution)/shard_map/all_to_all | solution.py:29
  131.3 0.0 collective-permute-start
  131.3 1.5 %collective-permute-done.other = f32[32,16,128]{2,1,0:T(8,128)S(1)} collective-permute-done((f32[32,16,128]{2,1,0:T(8,128)S(1)}, f32[32,16,128]{2,1,0:T(8,128)S(1)}, u32[]{:S(2)}, u32[]{:S(2)}) %collective-permute-start) | collective-permute-done | bytes 262176 | tf_op jit(solution)/shard_map/ppermute | solution.py:230
  132.8 0.0 copy-done.2
  132.8 0.7 copy-done.3
  133.5 7.3 %finish.1 = (f32[512,768]{1,0:T(8,128)}, f32[512,768]{1,0:T(8,128)}, f32[512,768]{1,0:T(8,128)}, f32[32,768]{1,0:T(8,128)}, f32[96,768]{1,0:T(8,128)}, /*index=5...) custom-call(s32[1]{0:T(128)} %bitcast.core, f32[32,16,128]{2,1,0:T(8,128)} %copy-done.2, f32[32,16,128]{2,1,0:T(8,128)} %copy-done.3, ...), custom_call_target="tpu_custom_call" | custom-call | tf_op jit(solution)/shard_map/finish/pallas_call | solution.py:133
  (36 shorter events, 0.4 us)
Async XLA Ops:
  0.6 1.4 copy-start.10
  1.7 1.4 %copy-start = (f32[1,512,768]{2,1,0:T(8,128)S(1)}, f32[1,512,768]{2,1,0:T(8,128)}, u32[]{:S(2)}) copy-start(f32[1,512,768]{2,1,0:T(8,128)} %param.16) | copy-start | bytes 4718596
  1.7 1.6 %copy-start.1 = (bf16[1,512,768]{2,1,0:T(8,128)(2,1)S(1)}, bf16[1,512,768]{2,1,0:T(8,128)(2,1)}, u32[]{:S(2)}) copy-start(bf16[1,512,768]{2,1,0:T(8,128)(2,1)} %param.15) | copy-start | bytes 2359300
  32.5 9.5 %copy-start.6 = (f32[2,32,32]{2,1,0:T(8,128)S(1)}, f32[2,32,32]{2,1,0:T(8,128)}, u32[]{:S(2)}) copy-start(f32[2,32,32]{2,1,0:T(8,128)} %param.20) | copy-start | bytes 24580
  32.5 9.6 %copy-start.7 = (f32[2,32,32]{2,1,0:T(8,128)S(1)}, f32[2,32,32]{2,1,0:T(8,128)}, u32[]{:S(2)}) copy-start(f32[2,32,32]{2,1,0:T(8,128)} %param.26) | copy-start | bytes 24580
  32.5 9.7 %copy-start.4 = (f32[768,32]{0,1:T(8,128)S(1)}, f32[768,32]{0,1:T(8,128)}, u32[]{:S(2)}) copy-start(f32[768,32]{0,1:T(8,128)} %param.19) | copy-start | bytes 294916
  32.5 9.7 %copy-start.5 = (f32[768,32]{0,1:T(8,128)S(1)}, f32[768,32]{0,1:T(8,128)}, u32[]{:S(2)}) copy-start(f32[768,32]{0,1:T(8,128)} %param.25) | copy-start | bytes 294916
  33.5 22.8 %all-to-all-start.1 = ((f32[8,120,128]{2,1,0:T(8,128)}), f32[8,120,128]{2,1,0:T(8,128)S(1)}, u32[]{:S(2)}, u32[]{:S(2)}) async-start(f32[8,120,128]{2,1,0:T(8,128)} %bitcast.7), calls=%async_computation.1 | async-start | bytes 983040 | tf_op jit(solution)/shard_map/all_to_all | solution.py:29
  42.0 19.6 %copy-start.8 = (f32[480]{0:T(512)S(1)}, f32[480]{0:T(512)}, u32[]{:S(2)}) copy-start(f32[480]{0:T(512)} %param.29) | copy-start | bytes 5764
  42.0 19.6 %copy-start.9 = (f32[480]{0:T(512)S(1)}, f32[480]{0:T(512)}, u32[]{:S(2)}) copy-start(f32[480]{0:T(512)} %param.28) | copy-start | bytes 5764
  57.1 13.4 %all-to-all-start.2 = ((f32[8,96,128]{2,1,0:T(8,128)}), f32[8,96,128]{2,1,0:T(8,128)S(1)}, u32[]{:S(2)}, u32[]{:S(2)}) async-start(f32[8,96,128]{2,1,0:T(8,128)} %bitcast.11), calls=%async_computation.2 | async-start | bytes 786432 | tf_op jit(solution)/shard_map/all_to_all | solution.py:29
  101.6 14.3 %all-to-all-start.5 = ((f32[32,8,128]{2,1,0:T(8,128)}), f32[32,8,128]{2,1,0:T(8,128)S(1)}, u32[]{:S(2)}, u32[]{:S(2)}) async-start(f32[32,8,128]{2,1,0:T(8,128)} %pad.23), calls=%async_computation.5 | async-start | bytes 262144 | tf_op jit(solution)/shard_map/all_to_all | solution.py:29
  131.3 1.5 %copy-start.2 = (f32[32,16,128]{2,1,0:T(8,128)}, f32[32,16,128]{2,1,0:T(8,128)S(1)}, u32[]{:S(2)}) copy-start(f32[32,16,128]{2,1,0:T(8,128)S(1)} %all_to_all.38.mine) | copy-start | bytes 786436
  131.3 1.5 %collective-permute-start = (f32[32,16,128]{2,1,0:T(8,128)S(1)}, f32[32,16,128]{2,1,0:T(8,128)S(1)}, u32[]{:S(2)}, u32[]{:S(2)}) collective-permute-start(f32[32,16,128]{2,1,0:T(8,128)S(1)} %all_to_all.38.mine), channel_id=1, source_target_pairs={{0,1},{1,0},{2,3},{3,2},{4,5},{5,4},{6,7},{7,6},{8,9},{9,8},{10,11... | collective-permute-start | bytes 786440 | tf_op jit(solution)/shard_map/ppermute | solution.py:230
  132.8 0.7 copy-start.3
